TPU v7x, 32 devices: a whole 2x2x4 slice. The times are simulated.
32 devices in a mesh: dp: 8 (over y, x, core), mp: 4 (over z).
Axes of the slice: x: 2, y: 2, z: 4, core: 2. Of those that a mesh axis runs over, the one named last changes fastest.
Arguments:
- inputs: bfloat16 [16, 512, 1024], P('dp'), may hold values from -6 to 6
- memory: bfloat16 [16, 512, 1024], P('dp'), may hold values from -6 to 6
- compressed_memory: bfloat16 [16, 512, 1024], P('dp'), may hold values from -6 to 6
- memory_fill: int32 [16], P('dp'), may hold values from 0 to 512, as said below
- compressed_fill: int32 [16], P('dp'), may hold values from 0 to 512, as said below
- first_gain: float32 [1024], replicated, may hold values from 0.5 to 1.5
- query_weight: bfloat16 [1024, 1024], P(None, 'mp'), may hold values from -0.1875 to 0.1875
- key_weight: bfloat16 [1024, 1024], P(None, 'mp'), may hold values from -0.1875 to 0.1875
- value_weight: bfloat16 [1024, 1024], P(None, 'mp'), may hold values from -0.1875 to 0.1875
- relative_bias: float32 [8, 22], P('mp'), may hold values from -1.5 to 1.5
- output_weight: bfloat16 [1024, 1024], P('mp'), may hold values from -1.5 to 1.5
- second_gain: float32 [1024], replicated, may hold values from 0.5 to 1.5
- up_weight: bfloat16 [1024, 4096], P(None, 'mp'), may hold values from -0.1875 to 0.1875
- down_weight: bfloat16 [4096, 1024], P('mp'), may hold values from -0.09375 to 0.09375
- compress_weight: bfloat16 [2048, 1024], P(None, 'mp'), may hold values from -0.125 to 0.125
- grad_output: bfloat16 [16, 512, 1024], P('dp'), may hold values from -6 to 6
- grad_compressed: bfloat16 [16, 256, 1024], P('dp', None, 'mp'), may hold values from -6 to 6
Outputs:
- outputs: bfloat16 [16, 512, 1024], P('dp')
- compressed: bfloat16 [16, 256, 1024], P('dp', None, 'mp')
- grad_inputs: bfloat16 [16, 512, 1024], P('dp')
- grad_first_gain: float32 [1024], replicated
- grad_query: float32 [1024, 1024], P(None, 'mp')
- grad_key: float32 [1024, 1024], P(None, 'mp')
- grad_value: float32 [1024, 1024], P(None, 'mp')
- grad_relative: float32 [8, 22], P('mp')
- grad_output_weight: float32 [1024, 1024], P('mp')
- grad_second_gain: float32 [1024], replicated
- grad_up: float32 [1024, 4096], P(None, 'mp')
- grad_down: float32 [4096, 1024], P('mp')
- grad_compress: float32 [2048, 1024], P(None, 'mp')
Inputs may be any that keep to these rules, and one draw needn't show every extreme that they name: `memory_fill`: some stream has a full memory and some stream an empty one. `compressed_fill`: some stream has a full compressed memory and some stream an empty one.
All inputs are finite; a program needn't handle non-finite values.
Results may differ from a plain program's by a relative error of at most 0.023.
Values sent between devices are 32-bit elements; how exact they have to be, the bound alone decides.
A program may use at most 320 MiB of HBM per device.

v0:
```python
import math
import jax
import jax.numpy as jnp
from jax import lax
from jax.sharding import PartitionSpec as P

reach_marks = (
    1,
    2,
    3,
    4,
    5,
    6,
    7,
    8,
    12,
    16,
    24,
    32,
    48,
    64,
    96,
    128,
    192,
    256,
    384,
    512,
    768,
    1024,
)
epsilon = 1e-06


def rms_scale(source, gain):
    return source * lax.rsqrt(jnp.mean(source * source, axis=-1, keepdims=True) + epsilon) * gain


def low_product(left, right):
    return jnp.dot(left, right, preferred_element_type=jnp.float32)


def weight_grad(left, right):
    return lax.dot_general(
        left, right, (((0,), (0,)), ((), ())), preferred_element_type=jnp.float32
    )


def back_product(left, right):
    return lax.dot_general(
        left, right, (((1,), (1,)), ((), ())), preferred_element_type=jnp.float32
    )


def gelu_tanh(source):
    return jax.nn.gelu(source, approximate=True)


def body(
    inputs,
    memory,
    compressed_memory,
    memory_fill,
    compressed_fill,
    first_gain,
    query_weight,
    key_weight,
    value_weight,
    relative_bias,
    output_weight,
    second_gain,
    up_weight,
    down_weight,
    compress_weight,
    grad_output,
    grad_compressed,
):
    seg_len = inputs.shape[1]
    mem_len = memory.shape[1]
    packed_len = compressed_memory.shape[1]
    model_width = inputs.shape[2]
    kept_count = packed_len + mem_len
    key_count = kept_count + seg_len
    heads_here = relative_bias.shape[0]
    head_dim = query_weight.shape[1] // heads_here
    compress_count = grad_compressed.shape[1]
    score_scale = 1.0 / math.sqrt(head_dim)
    distance = (
        jnp.arange(seg_len, dtype=jnp.int32)[:, None]
        + kept_count
        - jnp.arange(key_count, dtype=jnp.int32)[None, :]
    )
    causal = distance >= 0
    bias_table = jnp.zeros((heads_here, seg_len, key_count), jnp.float32)
    for position, mark_value in enumerate(reach_marks):
        bias_table = (
            bias_table
            + relative_bias[:, position][:, None, None]
            * (distance >= mark_value).astype(jnp.float32)[None]
        )

    def split_heads(source):
        return source.reshape(source.shape[0], heads_here, head_dim)

    def score_grid(queries, key_rows, allowed):
        raw_scores = (
            jnp.einsum(
                "shd,khd->hsk",
                split_heads(queries),
                split_heads(key_rows),
                preferred_element_type=jnp.float32,
            )
            * score_scale
            + bias_table
        )
        return jnp.where(allowed[None], raw_scores, -1e30)

    def attend(seg_rows, memory_rows, packed_rows, memory_count, packed_count):
        stacked = jnp.concatenate([packed_rows, memory_rows, seg_rows], axis=0).astype(jnp.float32)
        unit_rows = rms_scale(stacked, first_gain).astype(jnp.bfloat16)
        queries = low_product(unit_rows[kept_count:], query_weight).astype(jnp.bfloat16)
        key_rows = low_product(unit_rows, key_weight).astype(jnp.bfloat16)
        value_rows = low_product(unit_rows, value_weight).astype(jnp.bfloat16)
        valid_keys = jnp.concatenate(
            [
                jnp.arange(packed_len, dtype=jnp.int32) >= packed_len - packed_count,
                jnp.arange(mem_len, dtype=jnp.int32) >= mem_len - memory_count,
                jnp.ones((seg_len,), jnp.bool_),
            ]
        )
        allowed = causal & valid_keys[None, :]
        masked = score_grid(queries, key_rows, allowed)
        top_score = jnp.max(masked, axis=-1, keepdims=True)
        log_total = top_score + jnp.log(
            jnp.sum(jnp.exp(masked - top_score), axis=-1, keepdims=True)
        )
        prob_low = jnp.exp(masked - log_total).astype(jnp.bfloat16)
        mixed_heads = jnp.einsum(
            "hsk,khd->shd", prob_low, split_heads(value_rows), preferred_element_type=jnp.float32
        )
        mixed_heads = mixed_heads.reshape(seg_len, heads_here * head_dim).astype(jnp.bfloat16)
        attended = lax.psum(low_product(mixed_heads, output_weight), "mp")
        residual = seg_rows.astype(jnp.float32) + attended
        return (
            stacked,
            unit_rows,
            queries,
            key_rows,
            value_rows,
            allowed,
            log_total,
            mixed_heads,
            residual,
        )

    def feed(residual):
        ffn_input = rms_scale(residual, second_gain).astype(jnp.bfloat16)
        pre_act = low_product(ffn_input, up_weight)
        activated = gelu_tanh(pre_act).astype(jnp.bfloat16)
        return (ffn_input, pre_act, activated)

    def stream_step(totals, stream_item):
        seg_rows, memory_rows, packed_rows, memory_count, packed_count, grad_rows, grad_packed = (
            stream_item
        )
        saved = attend(seg_rows, memory_rows, packed_rows, memory_count, packed_count)
        ffn_input, pre_act, activated = feed(saved[8])
        branch_out = lax.psum(low_product(activated, down_weight), "mp")
        result = (saved[8] + branch_out).astype(jnp.bfloat16)
        again = lax.optimization_barrier((seg_rows, memory_rows, packed_rows, result))
        saved = attend(again[0], again[1], again[2], memory_count, packed_count)
        ffn_input, pre_act, activated = feed(saved[8])
        (
            stacked,
            unit_rows,
            queries,
            key_rows,
            value_rows,
            allowed,
            log_total,
            mixed_heads,
            residual,
        ) = saved
        slot_index = jnp.arange(mem_len, dtype=jnp.int32)
        live_rows = jnp.where(
            (slot_index >= mem_len - memory_count)[:, None],
            memory_rows,
            jnp.zeros_like(memory_rows),
        )
        evicted = live_rows.reshape(compress_count, 2 * model_width)
        packed_new = low_product(evicted, compress_weight).astype(jnp.bfloat16)
        grad_down = weight_grad(activated, grad_rows)
        _, gelu_back = jax.vjp(gelu_tanh, pre_act)
        grad_pre = gelu_back(back_product(grad_rows, down_weight))[0].astype(jnp.bfloat16)
        grad_up = weight_grad(ffn_input, grad_pre)
        grad_ffn_input = lax.psum(back_product(grad_pre, up_weight), "mp")
        _, second_back = jax.vjp(rms_scale, residual, second_gain)
        grad_res_norm, grad_second = second_back(grad_ffn_input)
        grad_residual = grad_rows.astype(jnp.float32) + grad_res_norm
        grad_attended = grad_residual.astype(jnp.bfloat16)
        grad_out_weight = weight_grad(mixed_heads, grad_attended)
        grad_mixed = back_product(grad_attended, output_weight).astype(jnp.bfloat16)
        masked = score_grid(queries, key_rows, allowed)
        attend_prob = jnp.exp(masked - log_total)
        grad_prob = jnp.einsum(
            "shd,khd->hsk",
            split_heads(grad_mixed),
            split_heads(value_rows),
            preferred_element_type=jnp.float32,
        )
        grad_score = (
            attend_prob * (grad_prob - jnp.sum(grad_prob * attend_prob, axis=-1, keepdims=True))
        ).astype(jnp.bfloat16)
        score_wide = grad_score.astype(jnp.float32)
        grad_relative = jnp.stack(
            [
                jnp.sum(jnp.where((distance >= mark_value)[None], score_wide, 0.0), axis=(1, 2))
                for mark_value in reach_marks
            ],
            axis=1,
        )
        grad_queries = (
            (
                jnp.einsum(
                    "hsk,khd->shd",
                    grad_score,
                    split_heads(key_rows),
                    preferred_element_type=jnp.float32,
                )
                * score_scale
            )
            .reshape(seg_len, heads_here * head_dim)
            .astype(jnp.bfloat16)
        )
        grad_keys = (
            (
                jnp.einsum(
                    "hsk,shd->khd",
                    grad_score,
                    split_heads(queries),
                    preferred_element_type=jnp.float32,
                )
                * score_scale
            )
            .reshape(key_count, heads_here * head_dim)
            .astype(jnp.bfloat16)
        )
        grad_values = (
            jnp.einsum(
                "hsk,shd->khd",
                attend_prob.astype(jnp.bfloat16),
                split_heads(grad_mixed),
                preferred_element_type=jnp.float32,
            )
            .reshape(key_count, heads_here * head_dim)
            .astype(jnp.bfloat16)
        )
        grad_query_w = weight_grad(unit_rows[kept_count:], grad_queries)
        grad_key_w = weight_grad(unit_rows, grad_keys)
        grad_value_w = weight_grad(unit_rows, grad_values)
        grad_unit = back_product(grad_keys, key_weight) + back_product(grad_values, value_weight)
        grad_unit_seg = grad_unit[kept_count:] + back_product(grad_queries, query_weight)
        _, kept_back = jax.vjp(rms_scale, stacked[:kept_count], first_gain)
        grad_first_kept = kept_back(grad_unit[:kept_count])[1]
        grad_unit_seg, grad_first_kept = lax.psum((grad_unit_seg, grad_first_kept), "mp")
        _, seg_back = jax.vjp(rms_scale, stacked[kept_count:], first_gain)
        grad_seg_norm, grad_first_seg = seg_back(grad_unit_seg)
        grad_seg = (grad_residual + grad_seg_norm).astype(jnp.bfloat16)
        grad_compress_w = weight_grad(evicted, grad_packed)
        gradients = (
            grad_first_kept + grad_first_seg,
            grad_query_w,
            grad_key_w,
            grad_value_w,
            grad_relative,
            grad_out_weight,
            grad_second,
            grad_up,
            grad_down,
            grad_compress_w,
        )
        totals = tuple((total + grad_item for total, grad_item in zip(totals, gradients)))
        return (totals, (result, packed_new, grad_seg))

    initial = tuple(
        (
            jnp.zeros(item.shape, jnp.float32)
            for item in (
                first_gain,
                query_weight,
                key_weight,
                value_weight,
                relative_bias,
                output_weight,
                second_gain,
                up_weight,
                down_weight,
                compress_weight,
            )
        )
    )
    stream_items = (
        inputs,
        memory,
        compressed_memory,
        memory_fill,
        compressed_fill,
        grad_output,
        grad_compressed,
    )
    totals, (results, packed_all, grad_all) = lax.scan(stream_step, initial, stream_items)
    totals = lax.psum(totals, "dp")
    return (results, packed_all, grad_all) + tuple(totals)


def solution(mesh):
    in_specs = (
        P("dp", None, None),
        P("dp", None, None),
        P("dp", None, None),
        P("dp"),
        P("dp"),
        P(),
        P(None, "mp"),
        P(None, "mp"),
        P(None, "mp"),
        P("mp", None),
        P("mp", None),
        P(),
        P(None, "mp"),
        P("mp", None),
        P(None, "mp"),
        P("dp", None, None),
        P("dp", None, "mp"),
    )
    out_specs = (
        P("dp", None, None),
        P("dp", None, "mp"),
        P("dp", None, None),
        P(),
        P(None, "mp"),
        P(None, "mp"),
        P(None, "mp"),
        P("mp", None),
        P("mp", None),
        P(),
        P(None, "mp"),
        P("mp", None),
        P(None, "mp"),
    )
    return jax.shard_map(body, mesh=mesh, in_specs=in_specs, out_specs=out_specs, check_vma=False)
```

profile of v0, /device:TPU:0, one launch (start us, length us, event | category | flops | bytes accessed | tf_op | source)
XLA Modules:
  0.0 1445.7 jit_solution(14084164727525014909)
XLA Ops:
  11.6 22.1 %fusion.144 = (f32[512,1536]{1,0:T(8,128)}, f32[512,1536]{1,0:T(8,128)}, f32[512,1536]{1,0:T(8,128)}, f32[512,1536]{1,0:T(8,128)}, f32[512,1536]{1,0:T(8,128)}, ...) fusion(s32[512]{0:T(512)S(1)} %iota_add_fusion), kind=kLoop, calls=%fused_computation.240 | loop fusion | flops 35389440 | bytes 69208064 | tf_op jit(solution)/shard_map/convert_element_type | solution.py:98
  33.8 1186.6 %while.40 = (s32[]{:T(128)}, f32[1024]{0:T(1024)S(1)}, f32[1024,256]{1,0:T(8,128)}, f32[1024,256]{1,0:T(8,128)}, f32[1024,256]{1,0:T(8,128)}, /*index=5*/f32[2,2...) while((s32[]{:T(128)}, f32[1024]{0:T(1024)S(1)}, ...), condition=%wide.region_45.46_spmd.clone.clone.clone.clone, body=%wide.region_0.45_spmd.clone.clone.clone.clone.sunk | while | flops 20195917824 | bytes 935102208 | solution.py:310
  50.8 12.6 fusion.370
  63.4 25.3 %multiply_add_fusion.4 = f32[2,512,1536]{2,1,0:T(8,128)} fusion(f32[512,1536]{1,0:T(8,128)} %get-tuple-element.2286, f32[2]{0:T(128)S(1)} %get-tuple-element.2287, f32[512,1536]{1,0:T(8,128)} %get-tuple-element.2284, f32[2]{0:T(128)S(1)} %get-tuple-element.2285, f32[512,1536]{1,0:T(8,128)} %get-tuple-element.2282, f32[2]{0:T(128)S(1)} %get-tuple-element.2283, ...), kind=kLoop, calls=%fused_computation.52.clone.1 | loop fusion | flops 67633152 | bytes 75497648 | tf_op jit(solution)/shard_map/add | solution.py:96
  98.1 89.3 %all-reduce.11.cloned.1.call-done = f32[512,1024]{1,0:T(8,128)} async-done(((f32[512,1024]{1,0:T(8,128)}), f32[512,1024]{1,0:T(8,128)}) %all-reduce.11.cloned.1.call-update) | async-done | bytes 2097168 | tf_op jit(solution)/shard_map/while/body/eval_jaxpr/psum | solution.py:141
  196.0 85.6 %all-reduce.13.cloned.1.call-done = f32[512,1024]{1,0:T(8,128)} async-done(((f32[512,1024]{1,0:T(8,128)}), f32[512,1024]{1,0:T(8,128)}) %all-reduce.13.cloned.1.call-update) | async-done | bytes 2097168 | tf_op jit(solution)/shard_map/while/body/eval_jaxpr/psum | solution.py:167
  324.9 67.0 %all-reduce.15.cloned.1.call-done = f32[512,1024]{1,0:T(8,128)} async-done(((f32[512,1024]{1,0:T(8,128)}), f32[512,1024]{1,0:T(8,128)}) %all-reduce.15.cloned.1.call-update) | async-done | bytes 2097168 | tf_op jit(solution)/shard_map/while/body/eval_jaxpr/psum | solution.py:141
  415.8 73.6 %all-reduce.17.cloned.1.call-done = f32[512,1024]{1,0:T(8,128)} async-done(((f32[512,1024]{1,0:T(8,128)}), f32[512,1024]{1,0:T(8,128)}) %all-reduce.17.cloned.1.call-update) | async-done | bytes 2097168 | tf_op jit(solution)/shard_map/while/body/eval_jaxpr/psum | solution.py:195
  501.3 25.2 %fusion.382 = (f32[2]{0:T(128)}, f32[2]{0:T(128)S(1)}, f32[2]{0:T(128)S(1)}, f32[2]{0:T(128)}, f32[2]{0:T(128)}, /*index=5*/f32[2]{0:T(128)}, f32[2]{0:T(128)}, ...) fusion(pred[512,1536]{1,0:T(8,128)(4,1)S(1)} %copy-done.19, ...), kind=kLoop, calls=%fused_computation.51.clone.1 | loop fusion | flops 64487408 | bytes 29892752 | tf_op jit(solution)/shard_map/while/body/eval_jaxpr/reduce_sum | solution.py:216
  535.3 6.7 fusion.388
  547.3 10.8 psum.174
  565.9 55.6 %all-reduce.19.cloned.1.call-done = f32[512,1024]{1,0:T(8,128)} async-done(((f32[512,1024]{1,0:T(8,128)}), f32[512,1024]{1,0:T(8,128)}) %all-reduce.19.cloned.1.call-update) | async-done | bytes 2097168 | tf_op jit(solution)/shard_map/while/body/eval_jaxpr/psum | solution.py:264
  645.4 12.6 fusion.370
  658.1 25.2 %multiply_add_fusion.4 = f32[2,512,1536]{2,1,0:T(8,128)} fusion(f32[512,1536]{1,0:T(8,128)} %get-tuple-element.2286, f32[2]{0:T(128)S(1)} %get-tuple-element.2287, f32[512,1536]{1,0:T(8,128)} %get-tuple-element.2284, f32[2]{0:T(128)S(1)} %get-tuple-element.2285, f32[512,1536]{1,0:T(8,128)} %get-tuple-element.2282, f32[2]{0:T(128)S(1)} %get-tuple-element.2283, ...), kind=kLoop, calls=%fused_computation.52.clone.1 | loop fusion | flops 67633152 | bytes 75497648 | tf_op jit(solution)/shard_map/add | solution.py:96
  692.6 85.6 %all-reduce.11.cloned.1.call-done = f32[512,1024]{1,0:T(8,128)} async-done(((f32[512,1024]{1,0:T(8,128)}), f32[512,1024]{1,0:T(8,128)}) %all-reduce.11.cloned.1.call-update) | async-done | bytes 2097168 | tf_op jit(solution)/shard_map/while/body/eval_jaxpr/psum | solution.py:141
  786.8 85.6 %all-reduce.13.cloned.1.call-done = f32[512,1024]{1,0:T(8,128)} async-done(((f32[512,1024]{1,0:T(8,128)}), f32[512,1024]{1,0:T(8,128)}) %all-reduce.13.cloned.1.call-update) | async-done | bytes 2097168 | tf_op jit(solution)/shard_map/while/body/eval_jaxpr/psum | solution.py:167
  917.1 65.4 %all-reduce.15.cloned.1.call-done = f32[512,1024]{1,0:T(8,128)} async-done(((f32[512,1024]{1,0:T(8,128)}), f32[512,1024]{1,0:T(8,128)}) %all-reduce.15.cloned.1.call-update) | async-done | bytes 2097168 | tf_op jit(solution)/shard_map/while/body/eval_jaxpr/psum | solution.py:141
  1011.0 69.0 %all-reduce.17.cloned.1.call-done = f32[512,1024]{1,0:T(8,128)} async-done(((f32[512,1024]{1,0:T(8,128)}), f32[512,1024]{1,0:T(8,128)}) %all-reduce.17.cloned.1.call-update) | async-done | bytes 2097168 | tf_op jit(solution)/shard_map/while/body/eval_jaxpr/psum | solution.py:195
  1091.9 25.2 %fusion.382 = (f32[2]{0:T(128)}, f32[2]{0:T(128)S(1)}, f32[2]{0:T(128)S(1)}, f32[2]{0:T(128)}, f32[2]{0:T(128)}, /*index=5*/f32[2]{0:T(128)}, f32[2]{0:T(128)}, ...) fusion(pred[512,1536]{1,0:T(8,128)(4,1)S(1)} %copy-done.19, ...), kind=kLoop, calls=%fused_computation.51.clone.1 | loop fusion | flops 64487408 | bytes 29892752 | tf_op jit(solution)/shard_map/while/body/eval_jaxpr/reduce_sum | solution.py:216
  1125.9 6.7 fusion.388
  1137.9 10.8 psum.174
  1158.2 53.9 %all-reduce.19.cloned.1.call-done = f32[512,1024]{1,0:T(8,128)} async-done(((f32[512,1024]{1,0:T(8,128)}), f32[512,1024]{1,0:T(8,128)}) %all-reduce.19.cloned.1.call-update) | async-done | bytes 2097168 | tf_op jit(solution)/shard_map/while/body/eval_jaxpr/psum | solution.py:264
  1221.0 14.8 %all-reduce = (f32[1024]{0:T(1024)}, f32[2,22]{1,0:T(2,128)}, f32[1024]{0:T(1024)}) all-reduce(f32[1024]{0:T(1024)S(1)} %get-tuple-element.2353, f32[2,22]{1,0:T(2,128)S(1)} %get-tuple-element.2357, f32[1024]{0:T(1024)S(1)} %get-tuple-element.2359), channel_id=1, replica_groups=mesh['dp'=8,'mp'=4] {'dp'}, use_global_device_ids=true, to_apply=%region_46.47 | all-reduce | flops 2092 | bytes 16736 | tf_op jit(solution)/shard_map/psum | solution.py:311
  1235.8 187.3 %all-reduce.9.cloned.1.call-done = (f32[1024,256]{1,0:T(8,128)}, f32[1024,256]{1,0:T(8,128)}, f32[1024,256]{1,0:T(8,128)}, f32[256,1024]{1,0:T(8,128)}, f32[1024...) async-done(((f32[1024,256]{1,0:T(8,128)}, f32[1024,256]{1,0:T(8,128)}, f32[1024,256]{1,0:T(8,128)}, f32[256,1024]{1,0:T(8,128)}, f32[1024,1024]{1,0:T(8,128)}, ...) | async-done | bytes 14680080 | tf_op jit(solution)/shard_map/psum | solution.py:311
  (643 shorter events, 307.1 us)
Async XLA Ops:
  11.6 22.2 %copy-start.66 = (f32[1024]{0:T(1024)S(1)}, f32[1024]{0:T(1024)}, u32[]{:S(2)}) copy-start(f32[1024]{0:T(1024)} %param.24) | copy-start | bytes 12292
  11.6 22.2 %copy-start.71 = (f32[1024]{0:T(1024)S(1)}, f32[1024]{0:T(1024)}, u32[]{:S(2)}) copy-start(f32[1024]{0:T(1024)} %param.30) | copy-start | bytes 12292
  11.6 22.2 %copy-start.94 = (s32[2]{0:T(128)S(1)}, s32[2]{0:T(128)}, u32[]{:S(2)}) copy-start(s32[2]{0:T(128)} %param.23) | copy-start | bytes 28
  34.0 153.4 %all-reduce.11.cloned.1.call-start = ((), (), s32[]{:S(2)}) async-start(), calls=%async_computation.1 | async-start | bytes 4194304 | tf_op jit(solution)/shard_map/while/body/eval_jaxpr/psum | solution.py:141
  63.4 25.4 %copy-start.9 = (pred[512,1536]{1,0:T(8,128)(4,1)}, pred[512,1536]{1,0:T(8,128)(4,1)S(1)}, u32[]{:S(2)}) copy-start(pred[512,1536]{1,0:T(8,128)(4,1)S(1)} %get-tuple-element.1992) | copy-start | bytes 2359300 | tf_op jit(solution)/shard_map/while
  98.0 183.6 %all-reduce.13.cloned.1.call-start = ((), (), s32[]{:S(2)}) async-start(), calls=%async_computation.2 | async-start | bytes 4194304 | tf_op jit(solution)/shard_map/while/body/eval_jaxpr/psum | solution.py:167
  196.0 195.9 %all-reduce.15.cloned.1.call-start = ((), (), s32[]{:S(2)}) async-start(), calls=%async_computation.3 | async-start | bytes 4194304 | tf_op jit(solution)/shard_map/while/body/eval_jaxpr/psum | solution.py:141
  306.3 183.1 %all-reduce.17.cloned.1.call-start = ((), (), s32[]{:S(2)}) async-start(), calls=%async_computation.4 | async-start | bytes 4194304 | tf_op jit(solution)/shard_map/while/body/eval_jaxpr/psum | solution.py:195
  403.8 217.7 %all-reduce.19.cloned.1.call-start = ((), (), s32[]{:S(2)}) async-start(), calls=%async_computation.5 | async-start | bytes 4194304 | tf_op jit(solution)/shard_map/while/body/eval_jaxpr/psum | solution.py:264
  496.2 33.5 %copy-start.37 = (bf16[2,128,1536]{2,1,0:T(8,128)(2,1)}, bf16[2,128,1536]{2,1,0:T(8,128)(2,1)S(1)}, u32[]{:S(2)}) copy-start(bf16[2,128,1536]{2,1,0:T(8,128)(2,1)S(1)} %convolution_convert_fusion.27) | copy-start | bytes 2359300 | tf_op jit(solution)/shard_map/while
  501.3 25.2 %copy-start.40 = (bf16[1536,256]{0,1:T(8,128)(2,1)S(1)}, bf16[1536,256]{0,1:T(8,128)(2,1)}, u32[]{:S(2)}) copy-start(bf16[1536,256]{0,1:T(8,128)(2,1)} %copy-done.39) | copy-start | bytes 2359300 | tf_op jit(solution)/shard_map/while
  565.9 61.2 %copy-start.68 = (f32[1024,256]{1,0:T(8,128)}, f32[1024,256]{1,0:T(8,128)S(1)}, u32[]{:S(2)}) copy-start(f32[1024,256]{1,0:T(8,128)S(1)} %convolution_add_fusion.14) | copy-start | bytes 3145732 | tf_op jit(solution)/shard_map/while
  628.6 149.5 %all-reduce.11.cloned.1.call-start = ((), (), s32[]{:S(2)}) async-start(), calls=%async_computation.1 | async-start | bytes 4194304 | tf_op jit(solution)/shard_map/while/body/eval_jaxpr/psum | solution.py:141
  658.1 25.2 %copy-start.9 = (pred[512,1536]{1,0:T(8,128)(4,1)}, pred[512,1536]{1,0:T(8,128)(4,1)S(1)}, u32[]{:S(2)}) copy-start(pred[512,1536]{1,0:T(8,128)(4,1)S(1)} %get-tuple-element.1992) | copy-start | bytes 2359300 | tf_op jit(solution)/shard_map/while
  692.5 179.8 %all-reduce.13.cloned.1.call-start = ((), (), s32[]{:S(2)}) async-start(), calls=%async_computation.2 | async-start | bytes 4194304 | tf_op jit(solution)/shard_map/while/body/eval_jaxpr/psum | solution.py:167
  786.8 195.8 %all-reduce.15.cloned.1.call-start = ((), (), s32[]{:S(2)}) async-start(), calls=%async_computation.3 | async-start | bytes 4194304 | tf_op jit(solution)/shard_map/while/body/eval_jaxpr/psum | solution.py:141
  896.9 183.1 %all-reduce.17.cloned.1.call-start = ((), (), s32[]{:S(2)}) async-start(), calls=%async_computation.4 | async-start | bytes 4194304 | tf_op jit(solution)/shard_map/while/body/eval_jaxpr/psum | solution.py:195
  994.4 217.8 %all-reduce.19.cloned.1.call-start = ((), (), s32[]{:S(2)}) async-start(), calls=%async_computation.5 | async-start | bytes 4194304 | tf_op jit(solution)/shard_map/while/body/eval_jaxpr/psum | solution.py:264
  1086.8 33.5 %copy-start.37 = (bf16[2,128,1536]{2,1,0:T(8,128)(2,1)}, bf16[2,128,1536]{2,1,0:T(8,128)(2,1)S(1)}, u32[]{:S(2)}) copy-start(bf16[2,128,1536]{2,1,0:T(8,128)(2,1)S(1)} %convolution_convert_fusion.27) | copy-start | bytes 2359300 | tf_op jit(solution)/shard_map/while
  1091.9 25.2 %copy-start.40 = (bf16[1536,256]{0,1:T(8,128)(2,1)S(1)}, bf16[1536,256]{0,1:T(8,128)(2,1)}, u32[]{:S(2)}) copy-start(bf16[1536,256]{0,1:T(8,128)(2,1)} %copy-done.39) | copy-start | bytes 2359300 | tf_op jit(solution)/shard_map/while
  1135.6 16.3 %copy-start.3 = (f32[512,1024]{1,0:T(8,128)S(1)}, f32[512,1024]{1,0:T(8,128)}, u32[]{:S(2)}) copy-start(f32[512,1024]{1,0:T(8,128)} %copy-done.2) | copy-start | bytes 6291460 | tf_op jit(solution)/shard_map/while
  1135.6 16.3 %copy-start.44 = (bf16[2,128,512]{2,1,0:T(8,128)(2,1)S(1)}, bf16[2,128,512]{2,1,0:T(8,128)(2,1)}, u32[]{:S(2)}) copy-start(bf16[2,128,512]{2,1,0:T(8,128)(2,1)} %copy-done.43) | copy-start | bytes 786436 | tf_op jit(solution)/shard_map/while
  1158.2 59.5 %copy-start.68 = (f32[1024,256]{1,0:T(8,128)}, f32[1024,256]{1,0:T(8,128)S(1)}, u32[]{:S(2)}) copy-start(f32[1024,256]{1,0:T(8,128)S(1)} %convolution_add_fusion.14) | copy-start | bytes 3145732 | tf_op jit(solution)/shard_map/while
  1220.4 202.7 %all-reduce.9.cloned.1.call-start = ((), (), s32[]{:S(2)}) async-start(), calls=%async_computation | async-start | bytes 29360128 | tf_op jit(solution)/shard_map/psum | solution.py:311
  (183 other events, 656.5 us)
Sparse Core Ops, SparseCore 0:
  98.2 89.1 all-reduce.10
  196.1 85.4 all-reduce.12
  306.4 85.4 all-reduce.14
  403.9 85.4 all-reduce.16
  535.4 86.0 all-reduce.18
  692.7 85.4 all-reduce.10
  786.9 85.4 all-reduce.12
  897.0 85.4 all-reduce.14
  994.5 85.4 all-reduce.16
  1126.0 86.1 all-reduce.18
Sparse Core Ops, SparseCore 1:
  1227.0 196.1 all-reduce.8
where the time goes:
time: 1450 us
  waiting for transfers between devices  919 us (63%)
  other arithmetic  246 us (17%)
  matrix products  127 us (9%)
  local copies, waits for them, and re-layouts  94.7 us (7%)
  blocking collectives  36.4 us (3%)
  between operations  15.9 us (1%)
    psum x4, waiting for transfers between devices, attend(): attended = lax.psum(low_product(mixed_heads, output_weight), 'mp')  307 us
    psum x1, waiting for transfers between devices, body(): totals = lax.psum(totals, 'dp')  187 us
    psum x2, waiting for transfers between devices, stream_step(): branch_out = lax.psum(low_product(activated, down_weight), 'mp')  171 us
    psum x2, waiting for transfers between devices, stream_step(): grad_ffn_input = lax.psum(back_product(grad_pre, up_weight), 'mp')  143 us
    psum x2, waiting for transfers between devices, stream_step(): lax.psum((grad_unit_seg, grad_first_kept), 'mp')  110 us
    reduce_sum x4, other arithmetic, stream_step(): jnp.sum(jnp.where((distance >= mark_value)[None], score_wide, 0.0), axis=...  63.7 us
    add x2, other arithmetic, body(): bias_table + relative_bias[:, position][:, None, None] * (distance >= mar...  50.5 us
    while x380, local copies, waits for them, and re-layouts  43.6 us
  transfers between devices with their start and end apart: 11, of which 11 were waited for; matrix products, arithmetic and copies ran while one was open for 7% of the time, Pallas kernels for 0%

commit v1 on v0

--- a/solution.py
+++ b/solution.py
@@ -164,7 +164,9 @@
         )
         saved = attend(seg_rows, memory_rows, packed_rows, memory_count, packed_count)
         ffn_input, pre_act, activated = feed(saved[8])
-        branch_out = lax.psum(low_product(activated, down_weight), "mp")
+        xs = low_product(activated, down_weight)
+        value_now = jax.lax.all_gather(xs, axis_name="mp")
+        branch_out = jnp.sum(value_now, 0)
         result = (saved[8] + branch_out).astype(jnp.bfloat16)
         again = lax.optimization_barrier((seg_rows, memory_rows, packed_rows, result))
         saved = attend(again[0], again[1], again[2], memory_count, packed_count)

time: 1450 us -> 1590 us (1.097)
  waiting for transfers between devices: 919 us -> 1040 us
    all_gather x0 -> x2, waiting for transfers between devices: none -> 297 us  [stream_step(): value_now = jax.lax.all_gather(xs, axis_name='mp')]
    psum x2 -> x0, waiting for transfers between devices: 171 us -> none  [stream_step(): branch_out = lax.psum(low_product(activated, down_weight), 'mp')]
  transfers between devices with their start and end apart: 11 -> 11, of which waited for: 11 -> 11; matrix products, arithmetic and copies ran while one was open for 7% -> 6% of each run, Pallas kernels for 0% -> 0%
where the time goes in v1:
time: 1590 us; the launch traced here: 1580 us
  waiting for transfers between devices  1040 us (65%)
  other arithmetic  257 us (16%)
  matrix products  127 us (8%)
  local copies, waits for them, and re-layouts  94.5 us (6%)
  blocking collectives  36.4 us (2%)
  between operations  15.9 us (1%)
    psum x4, waiting for transfers between devices, attend(): attended = lax.psum(low_product(mixed_heads, output_weight), 'mp')  306 us
    all_gather x2, waiting for transfers between devices, stream_step(): value_now = jax.lax.all_gather(xs, axis_name='mp')  297 us
    psum x1, waiting for transfers between devices, body(): totals = lax.psum(totals, 'dp')  187 us
    psum x2, waiting for transfers between devices, stream_step(): grad_ffn_input = lax.psum(back_product(grad_pre, up_weight), 'mp')  143 us
    psum x2, waiting for transfers between devices, stream_step(): lax.psum((grad_unit_seg, grad_first_kept), 'mp')  109 us
    reduce_sum x4, other arithmetic, stream_step(): jnp.sum(jnp.where((distance >= mark_value)[None], score_wide, 0.0), axis=...  63.7 us
    add x2, other arithmetic, body(): bias_table + relative_bias[:, position][:, None, None] * (distance >= mar...  50.5 us
    while x380, local copies, waits for them, and re-layouts  43.5 us
  transfers between devices with their start and end apart: 11, of which 11 were waited for; matrix products, arithmetic and copies ran while one was open for 6% of the time, Pallas kernels for 0%

profile of v1, /device:TPU:0, one launch (start us, length us, event | category | flops | bytes accessed | tf_op | source)
XLA Modules:
  0.0 1581.6 jit_solution(6699587995182090438)
XLA Ops:
  11.6 21.8 %fusion.144 = (f32[512,1536]{1,0:T(8,128)}, f32[512,1536]{1,0:T(8,128)}, f32[512,1536]{1,0:T(8,128)}, f32[512,1536]{1,0:T(8,128)}, f32[512,1536]{1,0:T(8,128)}, ...) fusion(s32[512]{0:T(512)S(1)} %iota_add_fusion), kind=kLoop, calls=%fused_computation.240 | loop fusion | flops 35389440 | bytes 69208064 | tf_op jit(solution)/shard_map/convert_element_type | solution.py:98
  33.5 1322.9 %while.40 = (s32[]{:T(128)}, f32[1024]{0:T(1024)S(1)}, f32[1024,256]{1,0:T(8,128)}, f32[1024,256]{1,0:T(8,128)}, f32[1024,256]{1,0:T(8,128)}, /*index=5*/f32[2,2...) while((s32[]{:T(128)}, f32[1024]{0:T(1024)S(1)}, ...), condition=%wide.region_45.46_spmd.clone.clone.clone.clone, body=%wide.region_0.45_spmd.clone.clone.clone.clone.sunk | while | flops 20196966400 | bytes 964462336 | solution.py:312
  50.5 12.6 fusion.370
  63.1 25.3 %multiply_add_fusion.4 = f32[2,512,1536]{2,1,0:T(8,128)} fusion(f32[512,1536]{1,0:T(8,128)} %get-tuple-element.2288, f32[2]{0:T(128)S(1)} %get-tuple-element.2289, f32[512,1536]{1,0:T(8,128)} %get-tuple-element.2286, f32[2]{0:T(128)S(1)} %get-tuple-element.2287, f32[512,1536]{1,0:T(8,128)} %get-tuple-element.2284, f32[2]{0:T(128)S(1)} %get-tuple-element.2285, ...), kind=kLoop, calls=%fused_computation.52.clone.1 | loop fusion | flops 67633152 | bytes 75497648 | tf_op jit(solution)/shard_map/add | solution.py:96
  97.7 89.3 %all-reduce.10.cloned.1.call-done = f32[512,1024]{1,0:T(8,128)} async-done(((f32[512,1024]{1,0:T(8,128)}), f32[512,1024]{1,0:T(8,128)}) %all-reduce.10.cloned.1.call-update) | async-done | bytes 2097168 | tf_op jit(solution)/shard_map/while/body/eval_jaxpr/psum | solution.py:141
  195.7 148.7 %all-gather.8.cloned.1.call-done = f32[2048,1024]{1,0:T(8,128)} async-done(((f32[512,1024]{1,0:T(8,128)}), f32[2048,1024]{1,0:T(8,128)}) %all-gather.8.cloned.1.call-update) | async-done | bytes 8388624 | tf_op jit(solution)/shard_map/while/body/eval_jaxpr/all_gather | solution.py:168
  393.5 66.4 %all-reduce.12.cloned.1.call-done = f32[512,1024]{1,0:T(8,128)} async-done(((f32[512,1024]{1,0:T(8,128)}), f32[512,1024]{1,0:T(8,128)}) %all-reduce.12.cloned.1.call-update) | async-done | bytes 2097168 | tf_op jit(solution)/shard_map/while/body/eval_jaxpr/psum | solution.py:141
  483.9 73.5 %all-reduce.14.cloned.1.call-done = f32[512,1024]{1,0:T(8,128)} async-done(((f32[512,1024]{1,0:T(8,128)}), f32[512,1024]{1,0:T(8,128)}) %all-reduce.14.cloned.1.call-update) | async-done | bytes 2097168 | tf_op jit(solution)/shard_map/while/body/eval_jaxpr/psum | solution.py:197
  569.3 25.2 %fusion.382 = (f32[2]{0:T(128)}, f32[2]{0:T(128)S(1)}, f32[2]{0:T(128)S(1)}, f32[2]{0:T(128)}, f32[2]{0:T(128)}, /*index=5*/f32[2]{0:T(128)}, f32[2]{0:T(128)}, ...) fusion(pred[512,1536]{1,0:T(8,128)(4,1)S(1)} %copy-done.19, ...), kind=kLoop, calls=%fused_computation.51.clone.1 | loop fusion | flops 64487408 | bytes 29892752 | tf_op jit(solution)/shard_map/while/body/eval_jaxpr/reduce_sum | solution.py:218
  603.3 6.7 fusion.388
  615.3 10.8 psum.158
  633.9 55.6 %all-reduce.16.cloned.1.call-done = f32[512,1024]{1,0:T(8,128)} async-done(((f32[512,1024]{1,0:T(8,128)}), f32[512,1024]{1,0:T(8,128)}) %all-reduce.16.cloned.1.call-update) | async-done | bytes 2097168 | tf_op jit(solution)/shard_map/while/body/eval_jaxpr/psum | solution.py:266
  713.4 12.6 fusion.370
  726.0 25.2 %multiply_add_fusion.4 = f32[2,512,1536]{2,1,0:T(8,128)} fusion(f32[512,1536]{1,0:T(8,128)} %get-tuple-element.2288, f32[2]{0:T(128)S(1)} %get-tuple-element.2289, f32[512,1536]{1,0:T(8,128)} %get-tuple-element.2286, f32[2]{0:T(128)S(1)} %get-tuple-element.2287, f32[512,1536]{1,0:T(8,128)} %get-tuple-element.2284, f32[2]{0:T(128)S(1)} %get-tuple-element.2285, ...), kind=kLoop, calls=%fused_computation.52.clone.1 | loop fusion | flops 67633152 | bytes 75497648 | tf_op jit(solution)/shard_map/add | solution.py:96
  760.5 85.6 %all-reduce.10.cloned.1.call-done = f32[512,1024]{1,0:T(8,128)} async-done(((f32[512,1024]{1,0:T(8,128)}), f32[512,1024]{1,0:T(8,128)}) %all-reduce.10.cloned.1.call-update) | async-done | bytes 2097168 | tf_op jit(solution)/shard_map/while/body/eval_jaxpr/psum | solution.py:141
  854.8 148.7 %all-gather.8.cloned.1.call-done = f32[2048,1024]{1,0:T(8,128)} async-done(((f32[512,1024]{1,0:T(8,128)}), f32[2048,1024]{1,0:T(8,128)}) %all-gather.8.cloned.1.call-update) | async-done | bytes 8388624 | tf_op jit(solution)/shard_map/while/body/eval_jaxpr/all_gather | solution.py:168
  1054.0 64.8 %all-reduce.12.cloned.1.call-done = f32[512,1024]{1,0:T(8,128)} async-done(((f32[512,1024]{1,0:T(8,128)}), f32[512,1024]{1,0:T(8,128)}) %all-reduce.12.cloned.1.call-update) | async-done | bytes 2097168 | tf_op jit(solution)/shard_map/while/body/eval_jaxpr/psum | solution.py:141
  1147.3 69.0 %all-reduce.14.cloned.1.call-done = f32[512,1024]{1,0:T(8,128)} async-done(((f32[512,1024]{1,0:T(8,128)}), f32[512,1024]{1,0:T(8,128)}) %all-reduce.14.cloned.1.call-update) | async-done | bytes 2097168 | tf_op jit(solution)/shard_map/while/body/eval_jaxpr/psum | solution.py:197
  1228.2 25.2 %fusion.382 = (f32[2]{0:T(128)}, f32[2]{0:T(128)S(1)}, f32[2]{0:T(128)S(1)}, f32[2]{0:T(128)}, f32[2]{0:T(128)}, /*index=5*/f32[2]{0:T(128)}, f32[2]{0:T(128)}, ...) fusion(pred[512,1536]{1,0:T(8,128)(4,1)S(1)} %copy-done.19, ...), kind=kLoop, calls=%fused_computation.51.clone.1 | loop fusion | flops 64487408 | bytes 29892752 | tf_op jit(solution)/shard_map/while/body/eval_jaxpr/reduce_sum | solution.py:218
  1262.2 6.7 fusion.388
  1274.2 10.8 psum.158
  1294.5 53.6 %all-reduce.16.cloned.1.call-done = f32[512,1024]{1,0:T(8,128)} async-done(((f32[512,1024]{1,0:T(8,128)}), f32[512,1024]{1,0:T(8,128)}) %all-reduce.16.cloned.1.call-update) | async-done | bytes 2097168 | tf_op jit(solution)/shard_map/while/body/eval_jaxpr/psum | solution.py:266
  1356.9 14.8 all-reduce
  1371.8 187.3 %all-reduce.8.cloned.1.call-done = (f32[1024,256]{1,0:T(8,128)}, f32[1024,256]{1,0:T(8,128)}, f32[1024,256]{1,0:T(8,128)}, f32[256,1024]{1,0:T(8,128)}, f32[1024...) async-done(((f32[1024,256]{1,0:T(8,128)}, f32[1024,256]{1,0:T(8,128)}, f32[1024,256]{1,0:T(8,128)}, f32[256,1024]{1,0:T(8,128)}, f32[1024,1024]{1,0:T(8,128)}, ...) | async-done | bytes 14680080 | tf_op jit(solution)/shard_map/psum | solution.py:313
  (645 shorter events, 318.9 us)
Async XLA Ops:
  11.6 21.9 %copy-start.66 = (f32[1024]{0:T(1024)S(1)}, f32[1024]{0:T(1024)}, u32[]{:S(2)}) copy-start(f32[1024]{0:T(1024)} %param.24) | copy-start | bytes 12292
  11.6 21.9 %copy-start.71 = (f32[1024]{0:T(1024)S(1)}, f32[1024]{0:T(1024)}, u32[]{:S(2)}) copy-start(f32[1024]{0:T(1024)} %param.30) | copy-start | bytes 12292
  11.6 21.9 %copy-start.94 = (s32[2]{0:T(128)S(1)}, s32[2]{0:T(128)}, u32[]{:S(2)}) copy-start(s32[2]{0:T(128)} %param.23) | copy-start | bytes 28
  33.7 153.3 %all-reduce.10.cloned.1.call-start = ((), (), s32[]{:S(2)}) async-start(), calls=%async_computation.1 | async-start | bytes 4194304 | tf_op jit(solution)/shard_map/while/body/eval_jaxpr/psum | solution.py:141
  63.1 25.3 %copy-start.9 = (pred[512,1536]{1,0:T(8,128)(4,1)}, pred[512,1536]{1,0:T(8,128)(4,1)S(1)}, u32[]{:S(2)}) copy-start(pred[512,1536]{1,0:T(8,128)(4,1)S(1)} %get-tuple-element.1992) | copy-start | bytes 2359300 | tf_op jit(solution)/shard_map/while
  97.6 246.8 %all-gather.8.cloned.1.call-start = ((), (), s32[]{:S(2)}) async-start(), calls=%async_computation.2 | async-start | bytes 10485760 | tf_op jit(solution)/shard_map/while/body/eval_jaxpr/all_gather | solution.py:168
  195.7 264.3 %all-reduce.12.cloned.1.call-start = ((), (), s32[]{:S(2)}) async-start(), calls=%async_computation.3 | async-start | bytes 4194304 | tf_op jit(solution)/shard_map/while/body/eval_jaxpr/psum | solution.py:141
  375.0 182.4 %all-reduce.14.cloned.1.call-start = ((), (), s32[]{:S(2)}) async-start(), calls=%async_computation.4 | async-start | bytes 4194304 | tf_op jit(solution)/shard_map/while/body/eval_jaxpr/psum | solution.py:197
  471.8 217.7 %all-reduce.16.cloned.1.call-start = ((), (), s32[]{:S(2)}) async-start(), calls=%async_computation.5 | async-start | bytes 4194304 | tf_op jit(solution)/shard_map/while/body/eval_jaxpr/psum | solution.py:266
  564.2 33.5 %copy-start.37 = (bf16[2,128,1536]{2,1,0:T(8,128)(2,1)}, bf16[2,128,1536]{2,1,0:T(8,128)(2,1)S(1)}, u32[]{:S(2)}) copy-start(bf16[2,128,1536]{2,1,0:T(8,128)(2,1)S(1)} %convolution_convert_fusion.27) | copy-start | bytes 2359300 | tf_op jit(solution)/shard_map/while
  569.3 25.2 %copy-start.40 = (bf16[1536,256]{0,1:T(8,128)(2,1)S(1)}, bf16[1536,256]{0,1:T(8,128)(2,1)}, u32[]{:S(2)}) copy-start(bf16[1536,256]{0,1:T(8,128)(2,1)} %copy-done.39) | copy-start | bytes 2359300 | tf_op jit(solution)/shard_map/while
  633.9 61.2 %copy-start.68 = (f32[1024,256]{1,0:T(8,128)}, f32[1024,256]{1,0:T(8,128)S(1)}, u32[]{:S(2)}) copy-start(f32[1024,256]{1,0:T(8,128)S(1)} %convolution_add_fusion.14) | copy-start | bytes 3145732 | tf_op jit(solution)/shard_map/while
  696.6 149.4 %all-reduce.10.cloned.1.call-start = ((), (), s32[]{:S(2)}) async-start(), calls=%async_computation.1 | async-start | bytes 4194304 | tf_op jit(solution)/shard_map/while/body/eval_jaxpr/psum | solution.py:141
  726.0 25.2 %copy-start.9 = (pred[512,1536]{1,0:T(8,128)(4,1)}, pred[512,1536]{1,0:T(8,128)(4,1)S(1)}, u32[]{:S(2)}) copy-start(pred[512,1536]{1,0:T(8,128)(4,1)S(1)} %get-tuple-element.1992) | copy-start | bytes 2359300 | tf_op jit(solution)/shard_map/while
  760.4 243.0 %all-gather.8.cloned.1.call-start = ((), (), s32[]{:S(2)}) async-start(), calls=%async_computation.2 | async-start | bytes 10485760 | tf_op jit(solution)/shard_map/while/body/eval_jaxpr/all_gather | solution.py:168
  854.7 264.1 %all-reduce.12.cloned.1.call-start = ((), (), s32[]{:S(2)}) async-start(), calls=%async_computation.3 | async-start | bytes 4194304 | tf_op jit(solution)/shard_map/while/body/eval_jaxpr/psum | solution.py:141
  1033.9 182.4 %all-reduce.14.cloned.1.call-start = ((), (), s32[]{:S(2)}) async-start(), calls=%async_computation.4 | async-start | bytes 4194304 | tf_op jit(solution)/shard_map/while/body/eval_jaxpr/psum | solution.py:197
  1130.7 217.4 %all-reduce.16.cloned.1.call-start = ((), (), s32[]{:S(2)}) async-start(), calls=%async_computation.5 | async-start | bytes 4194304 | tf_op jit(solution)/shard_map/while/body/eval_jaxpr/psum | solution.py:266
  1223.1 33.5 %copy-start.37 = (bf16[2,128,1536]{2,1,0:T(8,128)(2,1)}, bf16[2,128,1536]{2,1,0:T(8,128)(2,1)S(1)}, u32[]{:S(2)}) copy-start(bf16[2,128,1536]{2,1,0:T(8,128)(2,1)S(1)} %convolution_convert_fusion.27) | copy-start | bytes 2359300 | tf_op jit(solution)/shard_map/while
  1228.2 25.2 %copy-start.40 = (bf16[1536,256]{0,1:T(8,128)(2,1)S(1)}, bf16[1536,256]{0,1:T(8,128)(2,1)}, u32[]{:S(2)}) copy-start(bf16[1536,256]{0,1:T(8,128)(2,1)} %copy-done.39) | copy-start | bytes 2359300 | tf_op jit(solution)/shard_map/while
  1271.9 16.3 %copy-start.3 = (f32[512,1024]{1,0:T(8,128)S(1)}, f32[512,1024]{1,0:T(8,128)}, u32[]{:S(2)}) copy-start(f32[512,1024]{1,0:T(8,128)} %copy-done.2) | copy-start | bytes 6291460 | tf_op jit(solution)/shard_map/while
  1272.0 16.2 %copy-start.44 = (bf16[2,128,512]{2,1,0:T(8,128)(2,1)S(1)}, bf16[2,128,512]{2,1,0:T(8,128)(2,1)}, u32[]{:S(2)}) copy-start(bf16[2,128,512]{2,1,0:T(8,128)(2,1)} %copy-done.43) | copy-start | bytes 786436 | tf_op jit(solution)/shard_map/while
  1294.5 59.2 %copy-start.68 = (f32[1024,256]{1,0:T(8,128)}, f32[1024,256]{1,0:T(8,128)S(1)}, u32[]{:S(2)}) copy-start(f32[1024,256]{1,0:T(8,128)S(1)} %convolution_add_fusion.14) | copy-start | bytes 3145732 | tf_op jit(solution)/shard_map/while
  1356.3 202.7 %all-reduce.8.cloned.1.call-start = ((), (), s32[]{:S(2)}) async-start(), calls=%async_computation | async-start | bytes 29360128 | tf_op jit(solution)/shard_map/psum | solution.py:313
  (183 other events, 656.6 us)
Sparse Core Ops, SparseCore 0:
  97.8 89.1 all-reduce.9
  195.8 148.5 all-gather.7
  375.2 84.7 all-reduce.11
  471.9 85.4 all-reduce.13
  603.4 86.0 all-reduce.15
  760.6 85.4 all-reduce.9
  854.8 148.5 all-gather.7
  1034.1 84.7 all-reduce.11
  1130.8 85.4 all-reduce.13
  1262.3 85.7 all-reduce.15
Sparse Core Ops, SparseCore 1:
  1362.9 196.1 all-reduce.7
